TPU v7x, 128 devices: a whole 4x4x4 slice. The times are simulated.
128 devices in a mesh: expert: 8 (over y, z_lo), fsdp: 16 (over x, z_hi, core).
Axes of the slice: x: 4, y: 4, z: 4 (z_hi: 2, z_lo: 2; z = z_hi * 2 + z_lo), core: 2. Of those that a mesh axis runs over, the one named last changes fastest.
Arguments:
- tokens: bfloat16 [18432, 2048], P(('expert', 'fsdp')), may hold values from -6 to 6
- expert_ids: int32 [18432, 6], P(('expert', 'fsdp')), may hold values from 0 to 15, as said below
- combine: float32 [18432, 6], P(('expert', 'fsdp')), may hold values from 0.05 to 1
- gate_weight: bfloat16 [16, 1408, 2048], P('expert', 'fsdp'), may hold values from -0.125 to 0.125
- up_weight: bfloat16 [16, 1408, 2048], P('expert', 'fsdp'), may hold values from -0.125 to 0.125
- down_weight: bfloat16 [16, 1408, 2048], P('expert', 'fsdp'), may hold values from -0.15625 to 0.15625
Outputs:
- mixed: bfloat16 [18432, 2048], P(('expert', 'fsdp'))
Inputs may be any that keep to these rules, and one draw needn't show every extreme that they name: `expert_ids`: each row names 6 different experts. Within the 144 rows of each device no expert is named more than 72 times, and one and the same expert is named exactly 72 times by the rows of every device.
All inputs are finite; a program needn't handle non-finite values.
Results may differ from a plain program's by a relative error of at most 0.0058.
Values may be sent and summed in bfloat16 or wider, within the bound.
A program may use at most 128 MiB of HBM per device.

v0:
```python
import jax
import jax.numpy as jnp
from jax import lax
from jax.sharding import Mesh
from jax.sharding import PartitionSpec as P

CAP = 72


def gather_expert(piece, core):
    mine = lax.dynamic_index_in_dim(piece, core, 0, keepdims=False)
    other = lax.dynamic_index_in_dim(piece, 1 - core, 0, keepdims=False)
    got = lax.ppermute(other, "core", [(0, 1), (1, 0)])
    pair = jnp.stack([mine, got])
    return lax.all_gather(pair, "chip", axis=0, tiled=True).reshape(-1, piece.shape[-1])


def per_device(tokens, expert_ids, combine, gate_weight, up_weight, down_weight):
    core = lax.axis_index("core")
    per_group = gate_weight.shape[0]
    groups = lax.axis_size("expert")
    n_expert = per_group * groups
    tok_rows, top_k = expert_ids.shape
    model_width = tokens.shape[1]
    gate_full = gather_expert(gate_weight, core)
    up_full = gather_expert(up_weight, core)
    down_full = gather_expert(down_weight, core)
    flat_ids = expert_ids.reshape(-1)
    onehot = (flat_ids[:, None] == jnp.arange(n_expert, dtype=jnp.int32)[None, :]).astype(jnp.int32)
    earlier = jnp.cumsum(onehot, axis=0) - onehot
    rank_within = jnp.sum(earlier * onehot, axis=1)
    slot_index = flat_ids * CAP + rank_within
    source = jnp.arange(tok_rows * top_k, dtype=jnp.int32) // top_k
    outgoing = (
        jnp.zeros((n_expert * CAP, model_width), jnp.bfloat16).at[slot_index].set(tokens[source])
    )
    outgoing = outgoing.reshape(n_expert, CAP, model_width)
    arrived = lax.all_to_all(outgoing, ("expert", "core"), 0, 0, tiled=True)
    rows = arrived.reshape(n_expert * CAP, model_width)
    gate_pre = jnp.dot(rows, gate_full.T, preferred_element_type=jnp.float32)
    up_pre = jnp.dot(rows, up_full.T, preferred_element_type=jnp.float32)
    hidden = (jax.nn.silu(gate_pre) * up_pre).astype(jnp.bfloat16)
    produced = jnp.dot(hidden, down_full, preferred_element_type=jnp.float32).astype(jnp.bfloat16)
    produced = produced.reshape(n_expert, CAP, model_width)
    returned = lax.all_to_all(produced, ("expert", "core"), 0, 0, tiled=True)
    back_rows = returned.reshape(n_expert * CAP, model_width)[slot_index]
    weighted = (
        back_rows.astype(jnp.float32).reshape(tok_rows, top_k, model_width) * combine[:, :, None]
    )
    return jnp.sum(weighted, axis=1).astype(jnp.bfloat16)


def solution(mesh):
    groups = mesh.shape["expert"]
    chips = mesh.shape["fsdp"] // 2
    inner = Mesh(mesh.devices.reshape(groups, chips, 2), ("expert", "chip", "core"))
    rows = P(("expert", "chip", "core"), None)
    weights = P("expert", ("chip", "core"), None)
    return jax.shard_map(
        per_device,
        mesh=inner,
        in_specs=(rows, rows, rows, weights, weights, weights),
        out_specs=rows,
        check_vma=False,
    )
```

profile of v0, /device:TPU:49, one launch (start us, length us, event | category | flops | bytes accessed | tf_op | source)
XLA Modules:
  0.0 445.9 jit_solution(6090683395632843541)
XLA Ops:
  6.5 0.0 copy-start
  6.5 0.0 copy-start.1
  6.5 0.0 all-gather.4.cloned.1.call-start
  6.5 1.3 constant_dynamic-slice_fusion.2
  7.8 0.0 copy-start.2
  7.8 0.8 collective-permute-start
  8.6 1.3 collective-permute-done
  9.9 0.9 pad_maximum_fusion
  10.8 0.0 all-gather.4.cloned.1.call-update
  10.8 0.0 all-gather.6.cloned.1.call-start
  10.9 1.2 constant_dynamic-slice_fusion.1
  12.1 0.5 collective-permute-start.1
  12.5 1.3 collective-permute-done.1
  13.8 0.9 pad_maximum_fusion.1
  14.7 0.0 all-gather.6.cloned.1.call-update
  14.8 0.0 all-gather.8.cloned.1.call-start
  14.8 0.0 copy-done.1
  14.8 0.1 constant_dynamic-slice_fusion
  14.9 0.5 collective-permute-start.2
  15.3 1.3 collective-permute-done.2
  16.6 0.9 pad_maximum_fusion.2
  17.6 0.0 all-gather.8.cloned.1.call-update
  17.6 0.0 copy-done.2
  17.6 0.1 copy.14
  17.7 0.1 eq.22
  17.9 2.0 reduce-window.6
  19.9 0.3 slice_reduce_fusion
  20.2 0.1 copy.13
  20.3 0.1 mul.36
  20.5 0.1 bitcast_bitcast_fusion
  20.7 0.0 copy-done
  20.7 23.1 %scatter_custom_fusion = bf16[1152,2048]{1,0:T(8,128)(2,1)} fusion(s32[864]{0:T(1024)S(1)} %fusion.6, bf16[144,2048]{1,0:T(8,128)(2,1)S(1)} %copy-done, s32[1024]{0:T(1024)S(1)} %pad_clamp_fusion.1, bf16[]{:T(256)} %constant.40.clone.1), kind=kCustom, calls=%fused_computation.7 | custom fusion | bytes 4718594 | tf_op jit(solution)/shard_map/scatter | solution.py:35
  43.8 70.3 %all_to_all.10 = bf16[16,72,2048]{2,1,0:T(8,128)(2,1)} all-to-all(bf16[16,72,2048]{2,1,0:T(8,128)(2,1)} %bitcast.43), channel_id=1, replica_groups=mesh['expert'=8,'chip'=8,'core'=2] {'expert','core'}, dimensions={0} | all-to-all | bytes 9437184 | tf_op jit(solution)/shard_map/all_to_all | solution.py:38
  114.1 32.5 %all-gather.4.cloned.1.call-done = bf16[16,88,2048]{2,1,0:T(8,128)(2,1)} async-done(((bf16[2,88,2048]{2,1,0:T(8,128)(2,1)}), bf16[16,88,2048]{2,1,0:T(8,128)(2,1)}) %all-gather.4.cloned.1.call-update) | async-done | bytes 5767184 | tf_op jit(solution)/shard_map/all_gather | solution.py:15
  146.6 12.8 %fusion.8 = f32[1152,1408]{1,0:T(8,128)} fusion(bf16[1152,2048]{1,0:T(8,128)(2,1)} %bitcast.44, bf16[1408,2048]{1,0:T(8,128)(2,1)} %bitcast.51), kind=kOutput, calls=%fused_computation.40 | convolution fusion | flops 6643777536 | bytes 16973824 | tf_op jit(solution)/shard_map/dot_general | solution.py:40
  159.4 72.2 %all-gather.6.cloned.1.call-done = bf16[16,88,2048]{2,1,0:T(8,128)(2,1)} async-done(((bf16[2,88,2048]{2,1,0:T(8,128)(2,1)}), bf16[16,88,2048]{2,1,0:T(8,128)(2,1)}) %all-gather.6.cloned.1.call-update) | async-done | bytes 5767184 | tf_op jit(solution)/shard_map/all_gather | solution.py:15
  231.6 84.9 %all-gather.8.cloned.1.call-done = bf16[16,88,2048]{2,1,0:T(8,128)(2,1)} async-done(((bf16[2,88,2048]{2,1,0:T(8,128)(2,1)}), bf16[16,88,2048]{2,1,0:T(8,128)(2,1)}) %all-gather.8.cloned.1.call-update) | async-done | bytes 5767184 | tf_op jit(solution)/shard_map/all_gather | solution.py:15
  316.5 22.7 %convolution_convert_fusion = bf16[1152,2048]{1,0:T(8,128)(2,1)} fusion(bf16[1408,2048]{1,0:T(8,128)(2,1)} %bitcast.53, bf16[1152,2048]{1,0:T(8,128)(2,1)} %bitcast.45, bf16[1408,2048]{1,0:T(8,128)(2,1)} %bitcast.52, f32[1152,1408]{1,0:T(8,128)} %fusion.8), kind=kOutput, calls=%fused_computation.6 | convolution fusion | flops 13299646464 | bytes 27459584 | tf_op jit(solution)/shard_map/dot_general | solution.py:43
  339.3 0.0 copy-start.3
  339.3 6.6 %all-to-all-start.1 = ((bf16[16,72,2048]{2,1,0:T(8,128)(2,1)}), bf16[16,72,2048]{2,1,0:T(8,128)(2,1)}, u32[]{:S(2)}, u32[]{:S(2)}) async-start(bf16[16,72,2048]{2,1,0:T(8,128)(2,1)} %bitcast.46), calls=%async_computation.1 | async-start | bytes 9437184 | tf_op jit(solution)/shard_map/all_to_all | solution.py:45
  345.8 0.0 copy-done.3
  345.8 0.1 copy.17
  346.0 66.4 %all-to-all-done.1 = bf16[16,72,2048]{2,1,0:T(8,128)(2,1)} async-done(((bf16[16,72,2048]{2,1,0:T(8,128)(2,1)}), bf16[16,72,2048]{2,1,0:T(8,128)(2,1)}, u32[]{:S(2)}, u32[]{:S(2)}) %all-to-all-start.1) | async-done | bytes 4718624 | tf_op jit(solution)/shard_map/all_to_all | solution.py:45
  412.3 11.7 %gather_fusion = bf16[864,2048]{1,0:T(8,128)(2,1)} fusion(bf16[1152,2048]{1,0:T(8,128)(2,1)} %bitcast.13, s32[1024]{0:T(1024)S(1)} %pad_clamp_fusion), kind=kCustom, calls=%fused_computation.1 | custom fusion | bytes 7081344 | tf_op jit(solution)/shard_map/gather | solution.py:46
  424.0 7.1 %reshape.120 = f32[144,6,2048]{2,1,0:T(8,128)} reshape(bf16[864,2048]{1,0:T(8,128)(2,1)} %gather_fusion) | data formatting | bytes 10616832 | tf_op jit(solution)/shard_map/convert_element_type | solution.py:48
  431.2 8.2 %multiply_reduce_fusion = bf16[144,2048]{1,0:T(8,128)(2,1)} fusion(f32[144,6,2048]{2,1,0:T(8,128)} %reshape.120, f32[144,6]{1,0:T(8,128)S(1)} %copy.17), kind=kLoop, calls=%fused_computation.4 | loop fusion | flops 3244032 | bytes 7671168 | tf_op jit(solution)/shard_map/reduce_sum | solution.py:50
  (9 shorter events, 0.1 us)
Async XLA Ops:
  6.5 14.1 %copy-start = (bf16[144,2048]{1,0:T(8,128)(2,1)S(1)}, bf16[144,2048]{1,0:T(8,128)(2,1)}, u32[]{:S(2)}) copy-start(bf16[144,2048]{1,0:T(8,128)(2,1)} %param.6) | copy-start | bytes 1769476
  6.5 8.3 %copy-start.1 = (bf16[2,88,2048]{2,1,0:T(8,128)(2,1)S(1)}, bf16[2,88,2048]{2,1,0:T(8,128)(2,1)}, u32[]{:S(2)}) copy-start(bf16[2,88,2048]{2,1,0:T(8,128)(2,1)} %param.11) | copy-start | bytes 2162692
  6.5 140.1 %all-gather.4.cloned.1.call-start = ((), (), s32[]{:S(2)}) async-start(), calls=%async_computation.2 | async-start | bytes 6488064 | tf_op jit(solution)/shard_map/all_gather | solution.py:15
  7.8 9.8 %copy-start.2 = (s32[144,6]{0,1:T(8,128)S(1)}, s32[144,6]{0,1:T(8,128)}, u32[]{:S(2)}) copy-start(s32[144,6]{0,1:T(8,128)} %param.7) | copy-start | bytes 10372
  7.8 2.1 collective-permute-start
  10.8 220.7 %all-gather.6.cloned.1.call-start = ((), (), s32[]{:S(2)}) async-start(), calls=%async_computation.3 | async-start | bytes 6488064 | tf_op jit(solution)/shard_map/all_gather | solution.py:15
  12.1 1.8 collective-permute-start.1
  14.8 301.8 %all-gather.8.cloned.1.call-start = ((), (), s32[]{:S(2)}) async-start(), calls=%async_computation.4 | async-start | bytes 6488064 | tf_op jit(solution)/shard_map/all_gather | solution.py:15
  14.9 1.8 collective-permute-start.2
  339.3 6.6 %copy-start.3 = (f32[144,6]{0,1:T(8,128)S(1)}, f32[144,6]{0,1:T(8,128)}, u32[]{:S(2)}) copy-start(f32[144,6]{0,1:T(8,128)} %param.8) | copy-start | bytes 10372
  339.3 73.1 %all-to-all-start.1 = ((bf16[16,72,2048]{2,1,0:T(8,128)(2,1)}), bf16[16,72,2048]{2,1,0:T(8,128)(2,1)}, u32[]{:S(2)}, u32[]{:S(2)}) async-start(bf16[16,72,2048]{2,1,0:T(8,128)(2,1)} %bitcast.46), calls=%async_computation.1 | async-start | bytes 9437184 | tf_op jit(solution)/shard_map/all_to_all | solution.py:45
Sparse Core Ops, SparseCore 0:
  11.0 135.6 all-gather.3
  148.9 82.5 all-gather.5
  233.9 82.5 all-gather.7
where the time goes:
time: 446 us
  waiting for transfers between devices  260 us (58%)
  blocking collectives  70.3 us (16%)
  local copies, waits for them, and re-layouts  45.4 us (10%)
  matrix products  35.5 us (8%)
  between operations  13.3 us (3%)
  other arithmetic  13.2 us (3%)
  starting transfers between devices  8.33 us (2%)
    all_gather x3, waiting for transfers between devices, gather_expert(): lax.all_gather(pair, 'chip', axis=0, tiled=True)  190 us
    all_to_all x1, blocking collectives, per_device(): arrived = lax.all_to_all(outgoing, ('expert', 'core'), 0, 0, tiled=True)  70.3 us
    all_to_all x1, waiting for transfers between devices, per_device(): returned = lax.all_to_all(produced, ('expert', 'core'), 0, 0, tiled=True)  66.4 us
    scatter x1, local copies, waits for them, and re-layouts, per_device(): jnp.zeros((n_expert * CAP, model_width), jnp.bfloat16).at[slot_index]  23.1 us
    dot_general x1, matrix products, per_device(): jnp.dot(hidden, down_full, preferred_element_type=jnp.float32)  22.7 us
    dot_general x1, matrix products, per_device(): gate_pre = jnp.dot(rows, gate_full.T, preferred_element_type=jnp.float32)  12.8 us
    gather x1, local copies, waits for them, and re-layouts, per_device(): back_rows = returned.reshape(n_expert * CAP, model_width)[slot_index]  11.7 us
  transfers between devices with their start and end apart: 7, of which 7 were waited for; matrix products, arithmetic and copies ran while one was open for 9% of the time, Pallas kernels for 0%

commit v1 on v0

--- a/solution.py
+++ b/solution.py
@@ -12,7 +12,14 @@
     other = lax.dynamic_index_in_dim(piece, 1 - core, 0, keepdims=False)
     got = lax.ppermute(other, "core", [(0, 1), (1, 0)])
     pair = jnp.stack([mine, got])
-    return lax.all_gather(pair, "chip", axis=0, tiled=True).reshape(-1, piece.shape[-1])
+
+    def follow_the_bars(frame):
+        y1 = jnp.stack([frame for _ in range(lax.axis_size("chip"))])
+        base_arr = lax.all_to_all(y1, "chip", 0, 0)
+        answer = jnp.concatenate(base_arr, axis=0)
+        return answer
+
+    return follow_the_bars(pair).reshape(-1, piece.shape[-1])
 
 
 def per_device(tokens, expert_ids, combine, gate_weight, up_weight, down_weight):

time: 446 us -> 492 us (1.10)
  waiting for transfers between devices: 260 us -> 358 us
  blocking collectives: 70.3 us -> 0 us
  starting transfers between devices: 8.33 us -> 32.9 us
  between operations: 13.3 us -> 0.17 us
  local copies, waits for them, and re-layouts: 45.4 us -> 53.3 us
    all_to_all x0 -> x4, waiting for transfers between devices: none -> 287 us  [the longest x3 221 us: follow_the_bars(): base_arr = lax.all_to_all(y1, 'chip', 0, 0)]
    all_gather x3 -> x0, waiting for transfers between devices: 190 us -> none  [gather_expert(): lax.all_gather(pair, 'chip', axis=0, tiled=True)]
    all_to_all x1 -> x0, blocking collectives: 70.3 us -> none  [per_device(): arrived = lax.all_to_all(outgoing, ('expert', 'core'), 0, 0, tiled=True)]
    all_to_all x0 -> x4, starting transfers between devices: none -> 22.6 us  [the longest x3 16.4 us: follow_the_bars(): base_arr = lax.all_to_all(y1, 'chip', 0, 0)]
    another operation x0 -> x3, local copies, waits for them, and re-layouts: none -> 9.51 us  [follow_the_bars(): y1 = jnp.stack([frame for _ in range(lax.axis_size('chip'))])]
  transfers between devices with their start and end apart: 7 -> 8, of which waited for: 7 -> 8; matrix products, arithmetic and copies ran while one was open for 9% -> 3% of each run, Pallas kernels for 0% -> 0%
where the time goes in v1:
time: 492 us
  waiting for transfers between devices  358 us (73%)
  local copies, waits for them, and re-layouts  53.3 us (11%)
  matrix products  35.5 us (7%)
  starting transfers between devices  32.9 us (7%)
  other arithmetic  11.4 us (2%)
    all_to_all x3, waiting for transfers between devices, follow_the_bars(): base_arr = lax.all_to_all(y1, 'chip', 0, 0)  221 us
    all_to_all x1, waiting for transfers between devices, per_device(): returned = lax.all_to_all(produced, ('expert', 'core'), 0, 0, tiled=True)  67.4 us
    all_to_all x1, waiting for transfers between devices, per_device(): arrived = lax.all_to_all(outgoing, ('expert', 'core'), 0, 0, tiled=True)  65.5 us
    scatter x1, local copies, waits for them, and re-layouts, per_device(): jnp.zeros((n_expert * CAP, model_width), jnp.bfloat16).at[slot_index]  23.1 us
    dot_general x1, matrix products, per_device(): jnp.dot(hidden, down_full, preferred_element_type=jnp.float32)  22.7 us
    all_to_all x3, starting transfers between devices, follow_the_bars(): base_arr = lax.all_to_all(y1, 'chip', 0, 0)  16.4 us
    dot_general x1, matrix products, per_device(): gate_pre = jnp.dot(rows, gate_full.T, preferred_element_type=jnp.float32)  12.8 us
    gather x1, local copies, waits for them, and re-layouts, per_device(): back_rows = returned.reshape(n_expert * CAP, model_width)[slot_index]  11.7 us
  transfers between devices with their start and end apart: 8, of which 8 were waited for; matrix products, arithmetic and copies ran while one was open for 3% of the time, Pallas kernels for 0%

profile of v1, /device:TPU:49, one launch (start us, length us, event | category | flops | bytes accessed | tf_op | source)
XLA Modules:
  0.0 491.6 jit_solution(9438458804622632527)
XLA Ops:
  0.0 0.0 copy-start
  0.0 0.8 broadcast_multiply_fusion
  0.8 0.8 copy.9
  1.6 0.1 copy.8
  1.7 0.1 mul.36
  1.9 0.1 eq.22
  2.0 2.0 reduce-window.6
  4.0 0.3 slice_reduce_fusion
  4.3 0.1 bitcast_bitcast_fusion
  4.5 0.0 copy-done
  4.5 23.1 %scatter_custom_fusion = bf16[1152,2048]{1,0:T(8,128)(2,1)} fusion(s32[864]{0:T(1024)S(1)} %fusion.6, bf16[144,2048]{1,0:T(8,128)(2,1)S(1)} %copy-done, s32[1024]{0:T(1024)S(1)} %pad_clamp_fusion.1, bf16[]{:T(256)} %constant.40.clone.1), kind=kCustom, calls=%fused_computation.7 | custom fusion | bytes 4718594 | tf_op jit(solution)/shard_map/scatter | solution.py:42
  27.7 0.0 copy-start.2
  27.7 6.2 %all-to-all-start = ((bf16[16,72,2048]{2,1,0:T(8,128)(2,1)}), bf16[16,72,2048]{2,1,0:T(8,128)(2,1)}, u32[]{:S(2)}, u32[]{:S(2)}) async-start(bf16[16,72,2048]{2,1,0:T(8,128)(2,1)} %bitcast.43), calls=%async_computation | async-start | bytes 9437184 | tf_op jit(solution)/shard_map/all_to_all | solution.py:45
  33.8 0.0 copy-done.2
  33.8 0.1 constant_dynamic-slice_fusion
  33.9 0.4 collective-permute-start.2
  34.3 1.4 collective-permute-done.2
  35.8 0.1 pad_maximum_fusion.2
  35.8 65.5 %all-to-all-done = bf16[16,72,2048]{2,1,0:T(8,128)(2,1)} async-done(((bf16[16,72,2048]{2,1,0:T(8,128)(2,1)}), bf16[16,72,2048]{2,1,0:T(8,128)(2,1)}, u32[]{:S(2)}, u32[]{:S(2)}) %all-to-all-start) | async-done | bytes 4718624 | tf_op jit(solution)/shard_map/all_to_all | solution.py:45
  101.3 3.2 stack.26
  104.5 6.6 %all-to-all-start.3 = ((bf16[8,2,88,2048]{3,2,1,0:T(8,128)(2,1)}), bf16[8,2,88,2048]{3,2,1,0:T(8,128)(2,1)}, u32[]{:S(2)}, u32[]{:S(2)}) async-start(bf16[8,2,88,2048]{3,2,1,0:T(8,128)(2,1)} %stack.26), calls=%async_computation.3 | async-start | bytes 11534336 | tf_op jit(solution)/shard_map/all_to_all | solution.py:18
  111.1 0.0 copy-done.3
  111.1 0.1 constant_dynamic-slice_fusion.2
  111.2 0.6 collective-permute-start
  111.7 1.3 collective-permute-done
  113.0 0.1 pad_maximum_fusion
  113.1 78.3 %all-to-all-done.3 = bf16[8,2,88,2048]{3,2,1,0:T(8,128)(2,1)} async-done(((bf16[8,2,88,2048]{3,2,1,0:T(8,128)(2,1)}), bf16[8,2,88,2048]{3,2,1,0:T(8,128)(2,1)}, u32[]{:S(2)}, u32[]{:S(2)}) %all-to-all-start.3) | async-done | bytes 5767200 | tf_op jit(solution)/shard_map/all_to_all | solution.py:18
  191.4 3.2 stack.20
  194.5 5.1 %all-to-all-start.1 = ((bf16[8,2,88,2048]{3,2,1,0:T(8,128)(2,1)}), bf16[8,2,88,2048]{3,2,1,0:T(8,128)(2,1)}, u32[]{:S(2)}, u32[]{:S(2)}) async-start(bf16[8,2,88,2048]{3,2,1,0:T(8,128)(2,1)} %stack.20), calls=%async_computation.1 | async-start | bytes 11534336 | tf_op jit(solution)/shard_map/all_to_all | solution.py:18
  199.7 0.0 copy-done.4
  199.7 0.1 constant_dynamic-slice_fusion.1
  199.7 1.7 collective-permute-start.1
  201.4 1.3 collective-permute-done.1
  202.8 0.1 pad_maximum_fusion.1
  202.8 76.5 %all-to-all-done.1 = bf16[8,2,88,2048]{3,2,1,0:T(8,128)(2,1)} async-done(((bf16[8,2,88,2048]{3,2,1,0:T(8,128)(2,1)}), bf16[8,2,88,2048]{3,2,1,0:T(8,128)(2,1)}, u32[]{:S(2)}, u32[]{:S(2)}) %all-to-all-start.1) | async-done | bytes 5767200 | tf_op jit(solution)/shard_map/all_to_all | solution.py:18
  279.4 3.2 stack.23
  282.5 4.7 all-to-all-start.2
  287.2 12.8 %fusion.8 = f32[1152,1408]{1,0:T(8,128)} fusion(bf16[1152,2048]{1,0:T(8,128)(2,1)} %bitcast.2, bf16[1408,2048]{1,0:T(8,128)(2,1)} %bitcast.5), kind=kOutput, calls=%fused_computation.40 | convolution fusion | flops 6643777536 | bytes 16973824 | tf_op jit(solution)/shard_map/dot_general | solution.py:47
  300.0 66.6 %all-to-all-done.2 = bf16[8,2,88,2048]{3,2,1,0:T(8,128)(2,1)} async-done(((bf16[8,2,88,2048]{3,2,1,0:T(8,128)(2,1)}), bf16[8,2,88,2048]{3,2,1,0:T(8,128)(2,1)}, u32[]{:S(2)}, u32[]{:S(2)}) %all-to-all-start.2) | async-done | bytes 5767200 | tf_op jit(solution)/shard_map/all_to_all | solution.py:18
  366.6 22.7 %convolution_convert_fusion = bf16[1152,2048]{1,0:T(8,128)(2,1)} fusion(bf16[1408,2048]{1,0:T(8,128)(2,1)} %bitcast.11, bf16[1152,2048]{1,0:T(8,128)(2,1)} %bitcast.2, bf16[1408,2048]{1,0:T(8,128)(2,1)} %bitcast.8, f32[1152,1408]{1,0:T(8,128)} %fusion.8), kind=kOutput, calls=%fused_computation.6 | convolution fusion | flops 13299646464 | bytes 27459584 | tf_op jit(solution)/shard_map/dot_general | solution.py:50
  389.4 7.6 %all-to-all-start.4 = ((bf16[16,72,2048]{2,1,0:T(8,128)(2,1)}), bf16[16,72,2048]{2,1,0:T(8,128)(2,1)}, u32[]{:S(2)}, u32[]{:S(2)}) async-start(bf16[16,72,2048]{2,1,0:T(8,128)(2,1)} %bitcast.44), calls=%async_computation.4 | async-start | bytes 9437184 | tf_op jit(solution)/shard_map/all_to_all | solution.py:52
  397.0 0.0 copy-done.5
  397.0 0.1 copy.12
  397.2 67.4 %all-to-all-done.4 = bf16[16,72,2048]{2,1,0:T(8,128)(2,1)} async-done(((bf16[16,72,2048]{2,1,0:T(8,128)(2,1)}), bf16[16,72,2048]{2,1,0:T(8,128)(2,1)}, u32[]{:S(2)}, u32[]{:S(2)}) %all-to-all-start.4) | async-done | bytes 4718624 | tf_op jit(solution)/shard_map/all_to_all | solution.py:52
  464.5 11.7 %gather_fusion = bf16[864,2048]{1,0:T(8,128)(2,1)} fusion(bf16[1152,2048]{1,0:T(8,128)(2,1)} %bitcast.13, s32[1024]{0:T(1024)S(1)} %pad_clamp_fusion), kind=kCustom, calls=%fused_computation.1 | custom fusion | bytes 7081344 | tf_op jit(solution)/shard_map/gather | solution.py:53
  476.2 7.2 %reshape.114 = f32[144,6,2048]{2,1,0:T(8,128)} reshape(bf16[864,2048]{1,0:T(8,128)(2,1)} %gather_fusion) | data formatting | bytes 10616832 | tf_op jit(solution)/shard_map/convert_element_type | solution.py:55
  483.4 8.2 %multiply_reduce_fusion = bf16[144,2048]{1,0:T(8,128)(2,1)} fusion(f32[144,6,2048]{2,1,0:T(8,128)} %reshape.114, f32[144,6]{1,0:T(8,128)S(1)} %copy.12), kind=kLoop, calls=%fused_computation.4 | loop fusion | flops 3244032 | bytes 7671168 | tf_op jit(solution)/shard_map/reduce_sum | solution.py:57
  491.6 0.0 copy-done.1
  (12 shorter events, 0.1 us)
Async XLA Ops:
  0.0 4.5 copy-start
  27.7 6.2 %copy-start.2 = (bf16[2,88,2048]{2,1,0:T(8,128)(2,1)S(1)}, bf16[2,88,2048]{2,1,0:T(8,128)(2,1)}, u32[]{:S(2)}) copy-start(bf16[2,88,2048]{2,1,0:T(8,128)(2,1)} %param.11) | copy-start | bytes 2162692
  27.7 73.7 %all-to-all-start = ((bf16[16,72,2048]{2,1,0:T(8,128)(2,1)}), bf16[16,72,2048]{2,1,0:T(8,128)(2,1)}, u32[]{:S(2)}, u32[]{:S(2)}) async-start(bf16[16,72,2048]{2,1,0:T(8,128)(2,1)} %bitcast.43), calls=%async_computation | async-start | bytes 9437184 | tf_op jit(solution)/shard_map/all_to_all | solution.py:45
  33.9 1.9 collective-permute-start.2
  104.5 6.6 %copy-start.3 = (bf16[2,88,2048]{2,1,0:T(8,128)(2,1)S(1)}, bf16[2,88,2048]{2,1,0:T(8,128)(2,1)}, u32[]{:S(2)}) copy-start(bf16[2,88,2048]{2,1,0:T(8,128)(2,1)} %param.9) | copy-start | bytes 2162692
  104.5 86.9 %all-to-all-start.3 = ((bf16[8,2,88,2048]{3,2,1,0:T(8,128)(2,1)}), bf16[8,2,88,2048]{3,2,1,0:T(8,128)(2,1)}, u32[]{:S(2)}, u32[]{:S(2)}) async-start(bf16[8,2,88,2048]{3,2,1,0:T(8,128)(2,1)} %stack.26), calls=%async_computation.3 | async-start | bytes 11534336 | tf_op jit(solution)/shard_map/all_to_all | solution.py:18
  111.2 1.9 collective-permute-start
  194.5 5.1 %copy-start.4 = (bf16[2,88,2048]{2,1,0:T(8,128)(2,1)S(1)}, bf16[2,88,2048]{2,1,0:T(8,128)(2,1)}, u32[]{:S(2)}) copy-start(bf16[2,88,2048]{2,1,0:T(8,128)(2,1)} %param.10) | copy-start | bytes 2162692
  194.5 84.8 %all-to-all-start.1 = ((bf16[8,2,88,2048]{3,2,1,0:T(8,128)(2,1)}), bf16[8,2,88,2048]{3,2,1,0:T(8,128)(2,1)}, u32[]{:S(2)}, u32[]{:S(2)}) async-start(bf16[8,2,88,2048]{3,2,1,0:T(8,128)(2,1)} %stack.20), calls=%async_computation.1 | async-start | bytes 11534336 | tf_op jit(solution)/shard_map/all_to_all | solution.py:18
  199.7 3.0 collective-permute-start.1
  282.5 84.1 %all-to-all-start.2 = ((bf16[8,2,88,2048]{3,2,1,0:T(8,128)(2,1)}), bf16[8,2,88,2048]{3,2,1,0:T(8,128)(2,1)}, u32[]{:S(2)}, u32[]{:S(2)}) async-start(bf16[8,2,88,2048]{3,2,1,0:T(8,128)(2,1)} %stack.23), calls=%async_computation.2 | async-start | bytes 11534336 | tf_op jit(solution)/shard_map/all_to_all | solution.py:18
  389.4 7.7 %copy-start.5 = (f32[144,6]{0,1:T(8,128)S(1)}, f32[144,6]{0,1:T(8,128)}, u32[]{:S(2)}) copy-start(f32[144,6]{0,1:T(8,128)} %param.8) | copy-start | bytes 10372
  389.4 75.1 %all-to-all-start.4 = ((bf16[16,72,2048]{2,1,0:T(8,128)(2,1)}), bf16[16,72,2048]{2,1,0:T(8,128)(2,1)}, u32[]{:S(2)}, u32[]{:S(2)}) async-start(bf16[16,72,2048]{2,1,0:T(8,128)(2,1)} %bitcast.44), calls=%async_computation.4 | async-start | bytes 9437184 | tf_op jit(solution)/shard_map/all_to_all | solution.py:52
  476.2 15.4 %copy-start.1 = (bf16[144,2048]{1,0:T(8,128)(2,1)S(1)}, bf16[144,2048]{1,0:T(8,128)(2,1)}, u32[]{:S(2)}) copy-start(bf16[144,2048]{1,0:T(8,128)(2,1)} %param.6) | copy-start | bytes 1769476
